TPU v7x, 32 devices: a whole 2x2x4 slice. The times are simulated.
32 devices in a mesh: frames: 4 (over y, core), win: 8 (over z, x).
Axes of the slice: x: 2, y: 2, z: 4, core: 2. Of those that a mesh axis runs over, the one named last changes fastest.
Arguments:
- memberships: float32 [8, 256, 4096], P('win', 'frames'), as said below
- lag_times: int32 [8], P('win'), may hold values from 1 to 8, as said below
- segment_ids: int32 [8, 256], P('win'), may hold values from 0 to 7, never falling along the last dimension, each value on 1 to 128 neighbouring positions
- bias_codes: int32 [8, 4096], P('win'), may hold values from 0 to 511
Outputs:
- free_energy: float32 [4096], P('frames')
- log_multipliers: float32 [8, 4096], P('win', 'frames')
Inputs may be any that keep to these rules, and one draw needn't show every extreme that they name: Positive; each frame's memberships sum to one up to rounding. `lag_times`: some window's lag time is 8.
All inputs are finite; a program needn't handle non-finite values.
Results may differ from a plain program's by a relative error of at most 0.00041.
Values may be sent and summed in bfloat16 or wider, within the bound.
No kernel may reach another device: no remote copies, remote signals or barrier semaphores. Data moves between devices by JAX's collectives and lax.ppermute only.
A program may use at most 64 MiB of HBM per device.

v0:
```python
import jax
import jax.numpy as jnp
from jax import lax
from jax.sharding import PartitionSpec as P

LAGMAX = 8
ITERS = 2
bias_unit = 1.0 / 128.0


def shifted(block, axis, distance):
    devices = range(lax.axis_size(axis))
    route = [(i - distance, i) for i in devices if i - distance in devices]
    return lax.ppermute(block, axis, route)


def split_rows(block, frames_dev, lag_time, valid_all):
    width = frames_dev + LAGMAX
    number = block.shape[0] // width
    states = block.shape[1]
    shaped = block.reshape(number, width, states)
    current = shaped[:, :frames_dev].reshape(number * frames_dev, states)
    later = lax.dynamic_slice_in_dim(shaped, lag_time, frames_dev, 1).reshape(
        number * frames_dev, states
    )
    later = jnp.where(valid_all[:, None], later, jnp.zeros((), later.dtype))
    return (current, later)


def add_pair(accumulated, current, later, first, rows):
    current_cols = lax.dynamic_slice_in_dim(current, first, rows, 1)
    later_cols = lax.dynamic_slice_in_dim(later, first, rows, 1)
    accumulated = jnp.einsum("tr,ts->rs", current_cols, later, preferred_element_type=jnp.float32)
    return accumulated + jnp.einsum(
        "tr,ts->rs", later_cols, current, preferred_element_type=jnp.float32
    )


def shards(memberships, lag_times, segment_ids, bias_codes):
    member = memberships[0].astype(jnp.bfloat16)
    lag_time = lag_times[0]
    segment_row = segment_ids[0]
    frames_dev = member.shape[0]
    states = member.shape[1]
    frames_all = segment_row.shape[0]
    rows = states // lax.axis_size("frames")
    position = lax.axis_index("frames")
    first = position * rows
    heading = shifted(member[:LAGMAX], "frames", -1)
    extended = jnp.concatenate([member, heading], axis=0)
    segment_ext = jnp.concatenate([segment_row, jnp.full((LAGMAX,), -1, jnp.int32)])
    valid_all = segment_row == lax.dynamic_slice_in_dim(segment_ext, lag_time, frames_all, 0)
    empty = jnp.zeros((rows, states), jnp.float32)
    current, later = split_rows(
        lax.all_gather(extended, "frames", axis=0, tiled=True), frames_dev, lag_time, valid_all
    )
    sym_counts = add_pair(empty, current, later, first, rows)
    gammas = jnp.exp(-bias_codes[0].astype(jnp.float32) * bias_unit)
    gamma_rows = lax.dynamic_slice_in_dim(gammas, first, rows, 0)
    mult_rows = jnp.sum(sym_counts, axis=1) * 0.5
    mult_full = lax.all_gather(mult_rows, "frames", axis=0, tiled=True)
    window_total = jnp.sum(mult_full)
    count_rows = lax.psum(mult_rows, "win")
    weights = jnp.full((states,), 1.0 / states, jnp.float32)
    for sweep in range(ITERS):
        scaled = gammas * weights
        scaled_rows = lax.dynamic_slice_in_dim(scaled, first, rows, 0)
        denom = mult_rows[:, None] * scaled[None, :] + scaled_rows[:, None] * mult_full[None, :]
        ratios = sym_counts / denom
        new_rows = mult_rows * jnp.sum(ratios * scaled[None, :], axis=1)
        terms = gamma_rows * jnp.sum(ratios * mult_full[None, :], axis=1)
        term_rows = lax.psum(terms, "win")
        raw_rows = count_rows / term_rows
        if sweep + 1 < ITERS:
            raw_full, mult_full = (
                lax.all_gather(raw_rows, "frames", axis=0, tiled=True),
                lax.all_gather(new_rows, "frames", axis=0, tiled=True),
            )
        else:
            raw_full = lax.all_gather(raw_rows, "frames", axis=0, tiled=True)
        weights = raw_full / jnp.sum(raw_full)
        mult_rows = new_rows
    weight_rows = lax.dynamic_slice_in_dim(weights, first, rows, 0)
    free_energy = -jnp.log(states * weight_rows)
    log_multipliers = jnp.log(mult_rows * states / window_total)[None, :]
    return (free_energy, log_multipliers)


def solution(mesh):
    placed = (P("win", "frames", None), P("win"), P("win", None), P("win", None))
    return jax.shard_map(
        shards,
        mesh=mesh,
        in_specs=placed,
        out_specs=(P("frames"), P("win", "frames")),
        check_vma=False,
    )
```

profile of v0, /device:TPU:0, one launch (start us, length us, event | category | flops | bytes accessed | tf_op | source)
XLA Modules:
  0.0 147.7 jit_solution(16507466639481832255)
XLA Ops:
  7.2 0.0 all-gather.2.cloned.1.call-start
  7.2 1.3 convert_element_type.11
  8.5 1.3 collective-permute-start
  9.8 1.3 convert_bitcast_fusion
  11.1 0.6 collective-permute-done
  11.7 0.9 pad_maximum_fusion
  12.5 0.0 all-gather.2.cloned.1.call-update
  13.2 0.8 broadcast_multiply_fusion
  14.0 0.8 fusion.6
  14.8 25.7 %all-gather.2.cloned.1.call-done = bf16[288,4096]{1,0:T(8,128)(2,1)} async-done(((bf16[72,4096]{1,0:T(8,128)(2,1)}), bf16[288,4096]{1,0:T(8,128)(2,1)}) %all-gather.2.cloned.1.call-update) | async-done | bytes 2359312 | tf_op jit(solution)/shard_map/all_gather | solution.py:55
  40.5 2.9 %fusion.10 = (bf16[4,64,4096]{2,1,0:T(8,128)(2,1)S(1)}, bf16[4,64,4096]{2,1,0:T(8,128)(2,1)S(1)}) fusion(bf16[4,72,4096]{2,1,0:T(8,128)(2,1)} %bitcast.23, s32[]{:T(128)S(6)} %select_n.20), kind=kLoop, calls=%fused_computation.30 | loop fusion | bytes 8388612 | tf_op jit(solution)/shard_map/slice | solution.py:22
  43.4 0.0 copy-start.1
  43.4 0.4 bitcast_select_fusion
  43.8 0.9 copy-done.1
  44.8 8.1 %fusion.1 = f32[1024,4096]{1,0:T(8,128)} fusion(bf16[256,4096]{1,0:T(8,128)(2,1)S(1)} %bitcast_select_fusion, bf16[256,4096]{1,0:T(8,128)(2,1)S(1)} %bitcast.21, s32[]{:T(128)S(6)} %select_n.18), kind=kOutput, calls=%fused_computation.10 | convolution fusion | flops 2147483648 | bytes 19398660 | tf_op jit(solution)/shard_map/tr,ts->rs/dot_general | solution.py:33
  52.9 7.8 %fusion.11 = (f32[1024]{0:T(1024)S(1)}, f32[1024,4096]{1,0:T(8,128)S(1)}) fusion(f32[1024,4096]{1,0:T(8,128)} %fusion.1, bf16[256,4096]{1,0:T(8,128)(2,1)} %bitcast.22, bf16[256,4096]{1,0:T(8,128)(2,1)S(1)} %bitcast_select_fusion, s32[]{:T(128)S(6)} %select_n.18), kind=kOutput, calls=%fused_computation.31 | convolution fusion | flops 2155871232 | bytes 36179972 | tf_op jit(solution)/shard_map/tr,ts->rs/dot_general | solution.py:34
  60.7 0.0 copy-start
  60.7 5.2 %all_gather.16 = f32[4096]{0:T(1024)S(1)} all-gather(f32[1024]{0:T(1024)S(1)} %broadcast_multiply_fusion.1), channel_id=1, replica_groups=mesh['frames'=4,'win'=8] {'frames'}, dimensions={0}, use_global_device_ids=true | all-gather | bytes 20480 | tf_op jit(solution)/shard_map/all_gather | solution.py:61
  65.9 0.5 copy-done
  66.4 6.2 %multiply_reduce_fusion.2 = (f32[1024]{0:T(1024)S(1)}, f32[1024]{0:T(1024)S(1)}) fusion(f32[4096]{0:T(1024)S(1)} %all_gather.16, f32[4096]{0:T(1024)S(1)} %bitcast.26, f32[1024,4096]{1,0:T(8,128)S(1)} %get-tuple-element.13, f32[1024]{0:T(1024)S(1)} %dynamic-slice_multiply_fusion, f32[1024]{0:T(1024)S(1)} %broadcast_multiply_fusion.1), kind=kLoop, calls=%fused_computation.3 | loop fusion | flops 33552384 | bytes 16826368 | tf_op jit(solution)/shard_map/reduce_sum | solution.py:71
  72.6 5.2 %all_gather.18 = f32[4096]{0:T(1024)S(1)} all-gather(f32[1024]{0:T(1024)S(1)} %fusion.9), channel_id=1, replica_groups=mesh['frames'=4,'win'=8] {'frames'}, dimensions={0}, use_global_device_ids=true | all-gather | bytes 20480 | tf_op jit(solution)/shard_map/all_gather | solution.py:77
  77.8 21.6 %all-reduce.1 = (f32[1024]{0:T(1024)S(1)}, f32[1024]{0:T(1024)S(1)}) all-reduce(f32[1024]{0:T(1024)S(1)} %broadcast_multiply_fusion.1, f32[1024]{0:T(1024)S(1)} %mul.185), channel_id=1, replica_groups=mesh['frames'=4,'win'=8] {'win'}, use_global_device_ids=true, to_apply=%region_1.2 | all-reduce | flops 2048 | bytes 16384 | tf_op jit(solution)/shard_map/psum | solution.py:63
  99.4 5.2 %all_gather.17 = f32[4096]{0:T(1024)S(1)} all-gather(f32[1024]{0:T(1024)S(1)} %div.38), channel_id=1, replica_groups=mesh['frames'=4,'win'=8] {'frames'}, dimensions={0}, use_global_device_ids=true | all-gather | bytes 20480 | tf_op jit(solution)/shard_map/all_gather | solution.py:76
  104.6 0.6 reduce_sum.79
  105.2 0.6 reduce_sum.75
  105.8 0.7 divide_multiply_fusion
  106.5 9.0 %multiply_reduce_fusion = (f32[1024]{0:T(1024)S(1)}, f32[1024]{0:T(1024)S(1)}) fusion(f32[4096]{0:T(1024)S(1)} %divide_multiply_fusion, f32[4096]{0:T(1024)S(1)} %all_gather.18, f32[1024,4096]{1,0:T(8,128)} %copy-done, f32[1024]{0:T(1024)S(1)} %dynamic_slice.33, f32[1024]{0:T(1024)S(1)} %fusion.9), kind=kLoop, calls=%fused_computation | loop fusion | flops 33552384 | bytes 16826368 | tf_op jit(solution)/shard_map/reduce_sum | solution.py:70
  115.5 17.1 %psum.23 = f32[1024]{0:T(1024)S(1)} all-reduce(f32[1024]{0:T(1024)S(1)} %mul.193), channel_id=1, replica_groups=mesh['frames'=4,'win'=8] {'win'}, use_global_device_ids=true, to_apply=%region_7.8 | all-reduce | flops 1024 | bytes 8192 | tf_op jit(solution)/shard_map/psum | solution.py:72
  132.7 5.2 %all_gather.19 = f32[4096]{0:T(1024)S(1)} all-gather(f32[1024]{0:T(1024)S(1)} %div.42), channel_id=1, replica_groups=mesh['frames'=4,'win'=8] {'frames'}, dimensions={0}, use_global_device_ids=true | all-gather | bytes 20480 | tf_op jit(solution)/shard_map/all_gather | solution.py:80
  137.9 0.6 reduce_sum.77
  138.5 1.3 fusion.5
  139.7 1.2 divide_log_fusion
  (10 shorter events, 0.1 us)
Async XLA Ops:
  7.2 33.3 %all-gather.2.cloned.1.call-start = ((), (), s32[]{:S(2)}) async-start(), calls=%async_computation | async-start | bytes 2949120 | tf_op jit(solution)/shard_map/all_gather | solution.py:55
  8.5 3.1 %collective-permute-start = (bf16[8,4096]{1,0:T(8,128)(2,1)S(1)}, bf16[8,4096]{1,0:T(8,128)(2,1)S(1)}, u32[]{:S(2)}, u32[]{:S(2)}) collective-permute-start(bf16[8,4096]{1,0:T(8,128)(2,1)S(1)} %slice_bitcast_fusion), channel_id=1, source_target_pairs={{8,0},{16,8},{24,16},{9,1},{17,9},{25,17},{10,2},{18,10},{26,18},{... | collective-permute-start | bytes 196616 | tf_op jit(solution)/shard_map/ppermute | solution.py:14
  43.4 1.4 copy-start.1
  60.7 5.7 %copy-start = (f32[1024,4096]{1,0:T(8,128)}, f32[1024,4096]{1,0:T(8,128)S(1)}, u32[]{:S(2)}) copy-start(f32[1024,4096]{1,0:T(8,128)S(1)} %get-tuple-element.13) | copy-start | bytes 50331652
Sparse Core Ops, SparseCore 0:
  12.7 27.7 all-gather.1
where the time goes:
time: 148 us
  blocking collectives  59.6 us (40%)
  waiting for transfers between devices  26.2 us (18%)
  other arithmetic  25.5 us (17%)
  matrix products  15.9 us (11%)
  between operations  14.8 us (10%)
  local copies, waits for them, and re-layouts  4.38 us (3%)
    all_gather x1, waiting for transfers between devices, shards(): lax.all_gather(extended, 'frames', axis=0, tiled=True)  25.7 us
    psum x1, blocking collectives, shards(): count_rows = lax.psum(mult_rows, 'win')  21.6 us
    psum x1, blocking collectives, shards(): term_rows = lax.psum(terms, 'win')  17.1 us
    reduce_sum x1, other arithmetic, shards(): new_rows = mult_rows * jnp.sum(ratios * scaled[None, :], axis=1)  8.98 us
    dot_general x1, matrix products, add_pair(): jnp.einsum('tr,ts->rs', current_cols, later, preferred_element_type=jnp.f...  8.12 us
    dot_general x1, matrix products, add_pair(): jnp.einsum('tr,ts->rs', later_cols, current, preferred_element_type=jnp.f...  7.76 us
    reduce_sum x1, other arithmetic, shards(): terms = gamma_rows * jnp.sum(ratios * mult_full[None, :], axis=1)  6.19 us
    all_gather x1, blocking collectives, shards(): mult_full = lax.all_gather(mult_rows, 'frames', axis=0, tiled=True)  5.21 us
  transfers between devices with their start and end apart: 2, of which 2 were waited for; matrix products, arithmetic and copies ran while one was open for 2% of the time, Pallas kernels for 0%

commit v1 on v0

--- a/solution.py
+++ b/solution.py
@@ -1,3 +1,4 @@
+import functools
 import jax
 import jax.numpy as jnp
 from jax import lax
@@ -6,6 +7,22 @@
 LAGMAX = 8
 ITERS = 2
 bias_unit = 1.0 / 128.0
+
+
+def seats_all_carry(frame, d_out):
+    dev_n = lax.axis_size("frames")
+    leaves = [frame]
+    for no in [*range(1, dev_n)]:
+        leaves.append(
+            lax.ppermute(
+                leaves[no - 1], "frames", [(dev_i, (dev_i - 1) % dev_n) for dev_i in range(dev_n)]
+            )
+        )
+    all_values = jnp.concatenate(leaves, axis=d_out)
+    return jnp.roll(all_values, lax.axis_index("frames") * frame.shape[d_out], axis=d_out)
+
+
+watch_samples_up = functools.partial(seats_all_carry, d_out=0)
 
 
 def shifted(block, axis, distance):
@@ -51,9 +68,7 @@
     segment_ext = jnp.concatenate([segment_row, jnp.full((LAGMAX,), -1, jnp.int32)])
     valid_all = segment_row == lax.dynamic_slice_in_dim(segment_ext, lag_time, frames_all, 0)
     empty = jnp.zeros((rows, states), jnp.float32)
-    current, later = split_rows(
-        lax.all_gather(extended, "frames", axis=0, tiled=True), frames_dev, lag_time, valid_all
-    )
+    current, later = split_rows(watch_samples_up(extended), frames_dev, lag_time, valid_all)
     sym_counts = add_pair(empty, current, later, first, rows)
     gammas = jnp.exp(-bias_codes[0].astype(jnp.float32) * bias_unit)
     gamma_rows = lax.dynamic_slice_in_dim(gammas, first, rows, 0)

time: 148 us -> 142 us (0.959)
  between operations: 14.8 us -> 1.43 us
  starting transfers between devices: 1.33 us -> 8.52 us
  local copies, waits for them, and re-layouts: 4.38 us -> 11.2 us
  waiting for transfers between devices: 26.2 us -> 19.4 us
    all_gather x1 -> x0, waiting for transfers between devices: 25.7 us -> none  [shards(): lax.all_gather(extended, 'frames', axis=0, tiled=True)]
    ppermute x0 -> x3, waiting for transfers between devices: none -> 19.1 us  [seats_all_carry(): lax.ppermute(leaves[no - 1], 'frames', [(dev_i, (dev_i - 1) % dev_n) for...]
    ppermute x0 -> x3, starting transfers between devices: none -> 7.24 us  [seats_all_carry(): lax.ppermute(leaves[no - 1], 'frames', [(dev_i, (dev_i - 1) % dev_n) for...]
    unnamed x4 -> x12, local copies, waits for them, and re-layouts: 1.43 us -> 7.36 us
    convert_element_type x2 -> x0, other arithmetic: 2.56 us -> none  [shards(): member = memberships[0].astype(jnp.bfloat16)]
    dynamic_slice x0 -> x1, local copies, waits for them, and re-layouts: none -> 2.23 us  [seats_all_carry(): jnp.roll(all_values, lax.axis_index('frames') * frame.shape[d_out], axis=...]
    slice x1, local copies, waits for them, and re-layouts: 2.92 us -> 0.7 us  [split_rows(): current = shaped[:, :frames_dev].reshape(number * frames_dev, states)]
    unnamed x0 -> x1, other arithmetic: none -> 2.12 us
  transfers between devices with their start and end apart: 2 -> 4, of which waited for: 2 -> 4; matrix products, arithmetic and copies ran while one was open for 2% -> 3% of each run, Pallas kernels for 0% -> 0%
where the time goes in v1:
time: 142 us
  blocking collectives  60.9 us (43%)
  other arithmetic  24.2 us (17%)
  waiting for transfers between devices  19.4 us (14%)
  matrix products  15.9 us (11%)
  local copies, waits for them, and re-layouts  11.2 us (8%)
  starting transfers between devices  8.52 us (6%)
  between operations  1.43 us (1%)
    psum x1, blocking collectives, shards(): count_rows = lax.psum(mult_rows, 'win')  21.9 us
    ppermute x3, waiting for transfers between devices, seats_all_carry(): lax.ppermute(leaves[no - 1], 'frames', [(dev_i, (dev_i - 1) % dev_n) for...  19.1 us
    psum x1, blocking collectives, shards(): term_rows = lax.psum(terms, 'win')  17.1 us
    reduce_sum x1, other arithmetic, shards(): new_rows = mult_rows * jnp.sum(ratios * scaled[None, :], axis=1)  8.98 us
    dot_general x1, matrix products, add_pair(): jnp.einsum('tr,ts->rs', current_cols, later, preferred_element_type=jnp.f...  8.12 us
    dot_general x1, matrix products, add_pair(): jnp.einsum('tr,ts->rs', later_cols, current, preferred_element_type=jnp.f...  7.77 us
    unnamed x12, local copies, waits for them, and re-layouts  7.36 us
    ppermute x3, starting transfers between devices, seats_all_carry(): lax.ppermute(leaves[no - 1], 'frames', [(dev_i, (dev_i - 1) % dev_n) for...  7.24 us
  transfers between devices with their start and end apart: 4, of which 4 were waited for; matrix products, arithmetic and copies ran while one was open for 3% of the time, Pallas kernels for 0%

profile of v1, /device:TPU:0, one launch (start us, length us, event | category | flops | bytes accessed | tf_op | source)
XLA Modules:
  0.0 141.5 jit_solution(13948259230932229967)
XLA Ops:
  0.6 2.1 %constant_dynamic-update-slice_fusion.9 = (bf16[576,4096]{1,0:T(8,128)(2,1)}, bf16[1,64,4096]{2,1,0:T(8,128)(2,1)S(1)}) fusion(f32[1,64,4096]{2,1,0:T(8,128)} %param.4), kind=kLoop, calls=%fused_computation.22 | loop fusion | flops 262143 | bytes 2097152
  2.8 1.3 collective-permute-start
  4.7 0.8 fusion.8
  5.5 0.4 collective-permute-done
  5.9 3.4 %collective-permute-start.1 = (bf16[72,4096]{1,0:T(8,128)(2,1)S(1)}, bf16[72,4096]{1,0:T(8,128)(2,1)S(1)}, u32[]{:S(2)}, u32[]{:S(2)}) collective-permute-start(bf16[72,4096]{1,0:T(8,128)(2,1)S(1)} %pad_maximum_fusion), channel_id=1, source_target_pairs={{0,24},{8,0},{16,8},{24,16},{1,25},{9,1},{17,9},{25,17},{2,26},{10... | collective-permute-start | bytes 1769480 | tf_op jit(solution)/shard_map/ppermute | solution.py:17
  9.4 0.7 broadcast_multiply_fusion
  10.1 6.7 %collective-permute-done.1 = bf16[72,4096]{1,0:T(8,128)(2,1)S(1)} collective-permute-done((bf16[72,4096]{1,0:T(8,128)(2,1)S(1)}, bf16[72,4096]{1,0:T(8,128)(2,1)S(1)}, u32[]{:S(2)}, u32[]{:S(2)}) %collective-permute-start.1) | collective-permute-done | bytes 589856 | tf_op jit(solution)/shard_map/ppermute | solution.py:17
  16.8 1.9 %collective-permute-start.2 = (bf16[72,4096]{1,0:T(8,128)(2,1)S(1)}, bf16[72,4096]{1,0:T(8,128)(2,1)S(1)}, u32[]{:S(2)}, u32[]{:S(2)}) collective-permute-start(bf16[72,4096]{1,0:T(8,128)(2,1)S(1)} %collective-permute-done.1), channel_id=1, source_target_pairs={{0,24},{8,0},{16,8},{24,16},{1,25},{9,1},{17,9},{25,17},{2,26},{10... | collective-permute-start | bytes 1769480 | tf_op jit(solution)/shard_map/ppermute | solution.py:17
  18.7 0.6 constant_dynamic-update-slice_fusion.8
  19.3 6.8 %collective-permute-done.2 = bf16[72,4096]{1,0:T(8,128)(2,1)S(1)} collective-permute-done((bf16[72,4096]{1,0:T(8,128)(2,1)S(1)}, bf16[72,4096]{1,0:T(8,128)(2,1)S(1)}, u32[]{:S(2)}, u32[]{:S(2)}) %collective-permute-start.2) | collective-permute-done | bytes 589856 | tf_op jit(solution)/shard_map/ppermute | solution.py:17
  26.1 1.9 %collective-permute-start.3 = (bf16[72,4096]{1,0:T(8,128)(2,1)S(1)}, bf16[72,4096]{1,0:T(8,128)(2,1)S(1)}, u32[]{:S(2)}, u32[]{:S(2)}) collective-permute-start(bf16[72,4096]{1,0:T(8,128)(2,1)S(1)} %collective-permute-done.2), channel_id=1, source_target_pairs={{0,24},{8,0},{16,8},{24,16},{1,25},{9,1},{17,9},{25,17},{2,26},{10... | collective-permute-start | bytes 1769480 | tf_op jit(solution)/shard_map/ppermute | solution.py:17
  28.0 0.9 constant_dynamic-update-slice_fusion.7
  28.8 0.9 constant_dynamic-update-slice_fusion.6
  29.7 5.7 %collective-permute-done.3 = bf16[72,4096]{1,0:T(8,128)(2,1)S(1)} collective-permute-done((bf16[72,4096]{1,0:T(8,128)(2,1)S(1)}, bf16[72,4096]{1,0:T(8,128)(2,1)S(1)}, u32[]{:S(2)}, u32[]{:S(2)}) %collective-permute-start.3) | collective-permute-done | bytes 589856 | tf_op jit(solution)/shard_map/ppermute | solution.py:17
  35.4 0.9 constant_dynamic-update-slice_fusion.5
  36.3 0.8 constant_dynamic-update-slice_fusion.4
  37.1 0.6 constant_dynamic-update-slice_fusion.3
  37.7 0.9 constant_dynamic-update-slice_fusion.2
  38.6 0.9 constant_dynamic-update-slice_fusion.1
  39.4 0.9 constant_dynamic-update-slice_fusion
  40.3 2.2 %constant_dynamic-slice_fusion.2 = bf16[288,4096]{1,0:T(8,128)(2,1)S(1)} fusion(bf16[576,4096]{1,0:T(8,128)(2,1)} %constant_dynamic-update-slice_fusion, s32[]{:T(128)S(6)} %select_n.32), kind=kLoop, calls=%fused_computation.38 | loop fusion | bytes 4718596 | tf_op jit(solution)/shard_map/jit(_roll_dynamic)/dynamic_slice | solution.py:22
  42.5 0.7 fusion.10
  43.2 0.0 copy-start.1
  43.2 0.4 bitcast_select_fusion
  43.6 0.9 copy-done.1
  44.6 8.1 %fusion.1 = f32[1024,4096]{1,0:T(8,128)} fusion(bf16[256,4096]{1,0:T(8,128)(2,1)S(1)} %bitcast_select_fusion, bf16[256,4096]{1,0:T(8,128)(2,1)S(1)} %bitcast.23, s32[]{:T(128)S(6)} %select_n.33), kind=kOutput, calls=%fused_computation.10 | convolution fusion | flops 2147483648 | bytes 19398660 | tf_op jit(solution)/shard_map/tr,ts->rs/dot_general | solution.py:50
  52.7 7.8 %fusion.11 = (f32[1024]{0:T(1024)S(1)}, f32[1024,4096]{1,0:T(8,128)S(1)}) fusion(f32[1024,4096]{1,0:T(8,128)} %fusion.1, bf16[256,4096]{1,0:T(8,128)(2,1)} %bitcast.24, bf16[256,4096]{1,0:T(8,128)(2,1)S(1)} %bitcast_select_fusion, s32[]{:T(128)S(6)} %select_n.33), kind=kOutput, calls=%fused_computation.42 | convolution fusion | flops 2155871232 | bytes 36179972 | tf_op jit(solution)/shard_map/tr,ts->rs/dot_general | solution.py:51
  60.5 0.0 copy-start
  60.5 6.2 %all_gather.12 = f32[4096]{0:T(1024)S(1)} all-gather(f32[1024]{0:T(1024)S(1)} %broadcast_multiply_fusion.1), channel_id=1, replica_groups=mesh['frames'=4,'win'=8] {'frames'}, dimensions={0}, use_global_device_ids=true | all-gather | bytes 20480 | tf_op jit(solution)/shard_map/all_gather | solution.py:76
  66.8 6.2 %multiply_reduce_fusion.2 = (f32[1024]{0:T(1024)S(1)}, f32[1024]{0:T(1024)S(1)}) fusion(f32[4096]{0:T(1024)S(1)} %all_gather.12, f32[4096]{0:T(1024)S(1)} %bitcast.28, f32[1024,4096]{1,0:T(8,128)S(1)} %get-tuple-element.15, f32[1024]{0:T(1024)S(1)} %dynamic-slice_multiply_fusion, f32[1024]{0:T(1024)S(1)} %broadcast_multiply_fusion.1), kind=kLoop, calls=%fused_computation.3 | loop fusion | flops 33552384 | bytes 16826368 | tf_op jit(solution)/shard_map/reduce_sum | solution.py:86
  73.0 0.0 copy-done
  73.0 5.2 %all_gather.14 = f32[4096]{0:T(1024)S(1)} all-gather(f32[1024]{0:T(1024)S(1)} %fusion.9), channel_id=1, replica_groups=mesh['frames'=4,'win'=8] {'frames'}, dimensions={0}, use_global_device_ids=true | all-gather | bytes 20480 | tf_op jit(solution)/shard_map/all_gather | solution.py:92
  78.2 21.9 %all-reduce.1 = (f32[1024]{0:T(1024)S(1)}, f32[1024]{0:T(1024)S(1)}) all-reduce(f32[1024]{0:T(1024)S(1)} %broadcast_multiply_fusion.1, f32[1024]{0:T(1024)S(1)} %mul.189), channel_id=1, replica_groups=mesh['frames'=4,'win'=8] {'win'}, use_global_device_ids=true, to_apply=%region_1.2 | all-reduce | flops 2048 | bytes 16384 | tf_op jit(solution)/shard_map/psum | solution.py:78
  100.1 5.2 %all_gather.13 = f32[4096]{0:T(1024)S(1)} all-gather(f32[1024]{0:T(1024)S(1)} %div.38), channel_id=1, replica_groups=mesh['frames'=4,'win'=8] {'frames'}, dimensions={0}, use_global_device_ids=true | all-gather | bytes 20480 | tf_op jit(solution)/shard_map/all_gather | solution.py:91
  105.3 0.6 reduce_sum.79
  105.9 0.6 reduce_sum.75
  106.5 0.7 divide_multiply_fusion
  107.2 9.0 %multiply_reduce_fusion = (f32[1024]{0:T(1024)S(1)}, f32[1024]{0:T(1024)S(1)}) fusion(f32[4096]{0:T(1024)S(1)} %divide_multiply_fusion, f32[4096]{0:T(1024)S(1)} %all_gather.14, f32[1024,4096]{1,0:T(8,128)} %copy-done, f32[1024]{0:T(1024)S(1)} %dynamic_slice.38, f32[1024]{0:T(1024)S(1)} %fusion.9), kind=kLoop, calls=%fused_computation | loop fusion | flops 33552384 | bytes 16826368 | tf_op jit(solution)/shard_map/reduce_sum | solution.py:85
  116.2 17.1 %psum.23 = f32[1024]{0:T(1024)S(1)} all-reduce(f32[1024]{0:T(1024)S(1)} %mul.197), channel_id=1, replica_groups=mesh['frames'=4,'win'=8] {'win'}, use_global_device_ids=true, to_apply=%region_7.8 | all-reduce | flops 1024 | bytes 8192 | tf_op jit(solution)/shard_map/psum | solution.py:87
  133.3 5.2 %all_gather.15 = f32[4096]{0:T(1024)S(1)} all-gather(f32[1024]{0:T(1024)S(1)} %div.42), channel_id=1, replica_groups=mesh['frames'=4,'win'=8] {'frames'}, dimensions={0}, use_global_device_ids=true | all-gather | bytes 20480 | tf_op jit(solution)/shard_map/all_gather | solution.py:95
  138.5 0.6 reduce_sum.77
  139.1 1.3 fusion.5
  140.4 1.2 divide_log_fusion
  (11 shorter events, 0.1 us)
Async XLA Ops:
  2.8 3.1 %collective-permute-start = (bf16[8,4096]{1,0:T(8,128)(2,1)S(1)}, bf16[8,4096]{1,0:T(8,128)(2,1)S(1)}, u32[]{:S(2)}, u32[]{:S(2)}) collective-permute-start(bf16[8,4096]{1,0:T(8,128)(2,1)S(1)} %slice_bitcast_fusion), channel_id=1, source_target_pairs={{8,0},{16,8},{24,16},{9,1},{17,9},{25,17},{10,2},{18,10},{26,18},{... | collective-permute-start | bytes 196616 | tf_op jit(solution)/shard_map/ppermute | solution.py:31
  5.9 10.8 %collective-permute-start.1 = (bf16[72,4096]{1,0:T(8,128)(2,1)S(1)}, bf16[72,4096]{1,0:T(8,128)(2,1)S(1)}, u32[]{:S(2)}, u32[]{:S(2)}) collective-permute-start(bf16[72,4096]{1,0:T(8,128)(2,1)S(1)} %pad_maximum_fusion), channel_id=1, source_target_pairs={{0,24},{8,0},{16,8},{24,16},{1,25},{9,1},{17,9},{25,17},{2,26},{10... | collective-permute-start | bytes 1769480 | tf_op jit(solution)/shard_map/ppermute | solution.py:17
  16.8 9.3 %collective-permute-start.2 = (bf16[72,4096]{1,0:T(8,128)(2,1)S(1)}, bf16[72,4096]{1,0:T(8,128)(2,1)S(1)}, u32[]{:S(2)}, u32[]{:S(2)}) collective-permute-start(bf16[72,4096]{1,0:T(8,128)(2,1)S(1)} %collective-permute-done.1), channel_id=1, source_target_pairs={{0,24},{8,0},{16,8},{24,16},{1,25},{9,1},{17,9},{25,17},{2,26},{10... | collective-permute-start | bytes 1769480 | tf_op jit(solution)/shard_map/ppermute | solution.py:17
  26.1 9.3 %collective-permute-start.3 = (bf16[72,4096]{1,0:T(8,128)(2,1)S(1)}, bf16[72,4096]{1,0:T(8,128)(2,1)S(1)}, u32[]{:S(2)}, u32[]{:S(2)}) collective-permute-start(bf16[72,4096]{1,0:T(8,128)(2,1)S(1)} %collective-permute-done.2), channel_id=1, source_target_pairs={{0,24},{8,0},{16,8},{24,16},{1,25},{9,1},{17,9},{25,17},{2,26},{10... | collective-permute-start | bytes 1769480 | tf_op jit(solution)/shard_map/ppermute | solution.py:17
  43.2 1.4 copy-start.1
  60.5 12.5 %copy-start = (f32[1024,4096]{1,0:T(8,128)}, f32[1024,4096]{1,0:T(8,128)S(1)}, u32[]{:S(2)}) copy-start(f32[1024,4096]{1,0:T(8,128)S(1)} %get-tuple-element.15) | copy-start | bytes 50331652
